TPU v7x, 32 devices: a whole 2x2x4 slice. The times are simulated.
32 devices in a mesh: dp: 4 (over z), tensor: 8 (over y, x, core).
Axes of the slice: x: 2, y: 2, z: 4, core: 2. Of those that a mesh axis runs over, the one named last changes fastest.
Arguments:
- activations: bfloat16 [3072, 4096], P('dp', 'tensor'), may hold values from -6 to 6
- out_grads_t: bfloat16 [5504, 3072], P('tensor', 'dp'), may hold values from -6 to 6
- in_basis: bfloat16 [4096, 4096], P(None, 'tensor'), may hold values from -0.09375 to 0.09375
- out_basis_t: bfloat16 [5504, 5504], P('tensor'), may hold values from -0.078125 to 0.078125
- query_proj: bfloat16 [4, 5504, 4096], P(None, 'tensor', 'dp'), may hold values from -6 to 6
- eigvals: float32 [5504, 4096], P('tensor', 'dp'), may hold values from 0.05 to 5
- damping: float32 [1], replicated, may hold values from 0.05 to 0.2
- lengths: int32 [24], P('dp'), may hold values from 1 to 128, 1920 in all
Outputs:
- scores: float32 [24, 4], P('dp')
Inputs may be any that keep to these rules, and one draw needn't show every extreme that they name: `lengths`: the largest token count is exactly 128.
All inputs are finite; a program needn't handle non-finite values. No bound on the sum of `lengths` on one device may be relied on, other than what follows from the above.
Results may differ from a plain program's by a relative error of at most 0.006.
Values may be sent and summed in bfloat16 or wider, within the bound.
A program may use at most 128 MiB of HBM per device.

v0:
```python
import functools

import jax
import jax.numpy as jnp
from jax import lax
from jax.experimental import pallas as pl
from jax.experimental.pallas import tpu as pltpu
from jax.sharding import PartitionSpec as P


def generic(activations, out_grads_t, in_basis, out_basis_t, query_proj, eigvals, damping, lengths):
    bf16, f32 = jnp.bfloat16, jnp.float32
    seq_count = lengths.shape[0]
    full_act = lax.all_gather(activations, "tensor", axis=1, tiled=True)
    token_rows = full_act.shape[0]
    seq_len = token_rows // seq_count
    act_local = jnp.dot(full_act, in_basis, preferred_element_type=f32).astype(bf16)
    act_full = lax.all_gather(act_local, "tensor", axis=1, tiled=True)
    features = act_full.shape[1]
    act_proj = lax.all_to_all(act_full, "dp", split_axis=1, concat_axis=0, tiled=True)
    grad_full = jnp.dot(
        out_basis_t, lax.all_gather(out_grads_t, "tensor", axis=0, tiled=True), preferred_element_type=f32
    )
    position = lax.broadcasted_iota(jnp.int32, (seq_count, seq_len), 1)
    keep = (position < lengths[:, None]).astype(f32).reshape(1, token_rows)
    grad_local = (grad_full * keep).astype(bf16)
    grad_proj = lax.all_gather(grad_local, "dp", axis=1, tiled=True)
    scaled = (query_proj.astype(f32) / (eigvals + damping[0])).astype(bf16)
    mixed = jnp.einsum("td,qjd->qjt", act_proj, scaled, preferred_element_type=f32)
    weighted = mixed * grad_proj.astype(f32)[None, :, :]
    query_count, width, tokens = weighted.shape
    partial_value = jnp.sum(weighted.reshape(query_count, width, tokens // seq_len, seq_len), axis=(1, 3)).T
    totals = lax.psum(partial_value, ("dp", "tensor"))
    mine = lax.dynamic_slice_in_dim(totals, lax.axis_index("dp") * seq_count, seq_count, 0)
    norm_factor = (features * out_basis_t.shape[1] * seq_len) ** (-0.5)
    return mine * norm_factor


MESH = pl.DeviceIdType.MESH
CHUNK = 256


def kernel(
    planes, seq_len, act_ref, og_ref, in_ref, out_ref, query_ref, eig_ref, keep_ref, damp_ref, res_ref,
    og_all, act_all, in_b, out_b, scaled, eig, a_all, a_part, a_loc, a_acc, g_all, g_acc, csum, tiles, got_z, got_p,
    load_sem, gs_send, gs_recv, up_send, up_recv, dn_send, dn_recv, xp_send, xp_recv, xz_send, xz_recv,
    rz_send, rz_recv, rp_send, rp_recv,
):
    bf16, f32 = jnp.bfloat16, jnp.float32
    z, j = lax.axis_index("dp"), lax.axis_index("tensor")
    members = act_all.shape[0]
    rows, feats = act_ref.shape
    width, tokens = og_ref.shape
    depth = out_b.shape[1]
    queries, span = scaled.shape[0], scaled.shape[2]
    part = rows // members
    chunks = tokens // CHUNK
    jx = j + 2 - 4 * lax.rem(j // 2, 2)
    jy = j + 4 - 8 * (j // 4)
    jd = jx + 4 - 8 * (j // 4)

    def mate(k):
        return k + 1 - 2 * lax.rem(k, 2)

    jp = mate(j)

    loads = [
        pltpu.make_async_copy(og_ref, og_all.at[pl.ds(pl.multiple_of(j * width, 16), width), :], load_sem.at[0]),
        pltpu.make_async_copy(act_ref, act_all.at[j], load_sem.at[1]),
        pltpu.make_async_copy(query_ref, scaled, load_sem.at[2]),
        pltpu.make_async_copy(eig_ref, eig, load_sem.at[3]),
        pltpu.make_async_copy(out_ref, out_b, load_sem.at[4]),
        pltpu.make_async_copy(in_ref, in_b, load_sem.at[5]),
    ]
    for load in loads:
        load.start()

    barrier = pltpu.get_barrier_semaphore()
    for step in range(1, members):
        pl.semaphore_signal(barrier, inc=1, device_id={"tensor": lax.rem(j + step, members)}, device_id_type=MESH)
    for step in range(1, planes):
        pl.semaphore_signal(barrier, inc=1, device_id={"dp": lax.rem(z + step, planes)}, device_id_type=MESH)
    pl.semaphore_wait(barrier, members + planes - 2)

    cut = (width // 2 + 15) // 16 * 16

    def og_rows(h):
        return (0, width) if h is None else ((0, cut), (cut, width - cut))[h]

    def og_view(lanes):
        def view(k, h):
            first, size = og_rows(h)
            return og_all.at[pl.ds(pl.multiple_of(k * width + first, 16), size), lanes]

        return view

    def og_own(lanes):
        return lambda h: og_ref.at[pl.ds(*og_rows(h)), lanes]

    def act_view(k, h):
        if h is None:
            return act_all.at[k]
        return act_all.at[k, pl.ds(h * (rows // 2), rows // 2), :]

    def a_view(k, h):
        at = pl.ds(pl.multiple_of(k * part, 16), part)
        if h is None:
            return a_all.at[:, at, :]
        return a_all.at[pl.ds(h * (planes // 2), planes // 2), at, :]

    class Gather:
        def __init__(self, op, view, own):
            self.op, self.view, self.own = op, view, own
            self.plan = [
                (j, 0, jx), (j, 1, jx), (jy, 1, jx),
                (j, 1, jy), (j, 0, jy), (jx, 0, jy),
                (j, None, jp), (jx, None, jp), (jy, None, jp), (jd, 0, jp), (jd, 1, jp),
            ]
            self.landed = [
                (jx, 0), (jx, 1), (jd, 1),
                (jy, 1), (jy, 0), (jd, 0),
                (jp, None), (mate(jx), None), (mate(jy), None), (mate(jd), 0), (mate(jd), 1),
            ]

        def copy(self, slot):
            block, half, target = self.plan[slot]
            src = self.own(half) if slot in (0, 1, 3, 4, 6) else self.view(block, half)
            return pltpu.make_async_remote_copy(
                src_ref=src, dst_ref=self.view(block, half), send_sem=gs_send.at[self.op, slot],
                recv_sem=gs_recv.at[self.op, slot], device_id={"tensor": target}, device_id_type=MESH,
            )

        def start(self, *slots):
            for slot in slots:
                self.copy(slot).start()

        def arrive(self, *slots):
            for slot in slots:
                block, half = self.landed[slot]
                view = self.view(block, half)
                pltpu.make_async_remote_copy(
                    src_ref=view, dst_ref=view, send_sem=gs_send.at[self.op, slot],
                    recv_sem=gs_recv.at[self.op, slot], device_id={"tensor": jp}, device_id_type=MESH,
                ).wait_recv()

        def open(self):
            self.start(0, 3, 6)

        def extend(self):
            self.start(1, 4)

        def begin(self):
            self.start(0, 3, 1, 4, 6)

        def relay(self):
            self.arrive(0)
            self.start(5)
            self.arrive(3)
            self.start(2)

        def share_near(self):
            self.arrive(1)
            self.start(7)
            self.arrive(4)
            self.start(8)

        def share_far(self):
            self.arrive(5)
            self.start(9)
            self.arrive(2)
            self.start(10)

        def drain(self):
            for slot in range(len(self.plan)):
                self.copy(slot).wait_send()

    def act_own(h):
        return act_ref if h is None else act_ref.at[pl.ds(h * (rows // 2), rows // 2), :]

    early, late = pl.ds(0, CHUNK), pl.ds(CHUNK, tokens - CHUNK)
    og = Gather(0, og_view(early), og_own(early))
    act = Gather(1, act_view, act_own)
    more = Gather(3, og_view(late), og_own(late))
    acts = Gather(2, a_view, lambda h: a_view(j, h))

    og.begin()
    csum[...] = jnp.zeros_like(csum)

    loads[2].wait()
    loads[3].wait()
    step_rows = 16

    def scale(i, carry):
        at = pl.ds(pl.multiple_of(i * step_rows, step_rows), step_rows)
        below = eig[at, :] + damp_ref[0]
        for q in range(queries):
            scaled[q, at, :] = (scaled[q, at, :].astype(f32) / below).astype(bf16)
        return carry

    lax.fori_loop(0, width // step_rows, scale, 0)

    og.relay()
    act.begin()
    og.share_near()
    og.share_far()
    og.arrive(6, 7, 8, 9, 10)
    loads[0].wait()
    loads[4].wait()

    def up(block, n):
        return pltpu.make_async_remote_copy(
            src_ref=g_all.at[block, n], dst_ref=g_all.at[block, n], send_sem=up_send.at[block, n],
            recv_sem=up_recv.at[block, n], device_id={"dp": lax.rem(z + 1, planes)}, device_id_type=MESH,
        )

    def down(block, n):
        return pltpu.make_async_remote_copy(
            src_ref=g_all.at[block, n], dst_ref=g_all.at[block, n], send_sem=dn_send.at[block, n],
            recv_sem=dn_recv.at[block, n], device_id={"dp": lax.rem(z + planes - 1, planes)}, device_id_type=MESH,
        )

    top, bottom = z == planes - 1, z == 0

    def service(level, n):
        @pl.when(z - level >= 0)
        def _():
            up(z - level, n).wait_recv()

        @pl.when((z - level >= 0) & (z < planes - 1))
        def _():
            up(z - level, n).start()

        @pl.when(z + level < planes)
        def _():
            down(z + level, n).wait_recv()

        @pl.when((z + level < planes) & (z > 0))
        def _():
            down(z + level, n).start()

    k_tile = 3 * CHUNK
    k_full = depth // k_tile

    def project(n, carry):
        at = pl.ds(pl.multiple_of(n * CHUNK, CHUNK), CHUNK)
        k_rest = depth - k_full * k_tile
        if k_rest:
            g_acc[...] = jnp.dot(
                out_b[:, pl.ds(k_full * k_tile, k_rest)], og_all[pl.ds(k_full * k_tile, k_rest), at],
                preferred_element_type=f32,
            )
        else:
            g_acc[...] = jnp.zeros_like(g_acc)

        def inner(k, c):
            deep = pl.ds(pl.multiple_of(k * k_tile, k_tile), k_tile)
            g_acc[...] += jnp.dot(out_b[:, deep], og_all[deep, at], preferred_element_type=f32)
            return c

        lax.fori_loop(0, k_full, inner, 0)
        g_all[z, n] = (g_acc[...] * keep_ref[0:1, at]).astype(bf16)

        @pl.when(z < planes - 1)
        def _():
            up(z, n).start()

        @pl.when(z > 0)
        def _():
            down(z, n).start()

        return carry

    project(0, 0)

    a_acc[...] = jnp.zeros_like(a_acc)
    loads[1].wait()
    loads[5].wait()

    def contract(first):
        def body(i, carry):
            k = first + i * (mate(first) - first)
            deep = pl.ds(pl.multiple_of(k * feats, feats), feats)
            a_acc[...] += jnp.dot(act_all[k], in_b[deep, :], preferred_element_type=f32)
            return carry

        lax.fori_loop(0, 2, body, 0)

    act.relay()
    more.open()
    act.arrive(6)
    contract(j)
    act.share_near()
    service(1, 0)
    act.arrive(7)
    contract(jx)
    act.arrive(8)
    contract(jy)
    service(2, 0)
    act.share_far()
    act.arrive(9, 10)
    contract(jd)
    a_loc[...] = a_acc[...].astype(bf16)

    def spread(to):
        return pltpu.make_async_remote_copy(
            src_ref=a_loc.at[pl.ds(pl.multiple_of(to * part, 16), part), :],
            dst_ref=a_part.at[j], send_sem=xp_send.at[to], recv_sem=xp_recv.at[j],
            device_id={"tensor": to}, device_id_type=MESH,
        )

    def spread_from(k):
        return pltpu.make_async_remote_copy(
            src_ref=a_part.at[k], dst_ref=a_part.at[k], send_sem=xp_send.at[k], recv_sem=xp_recv.at[k],
            device_id={"tensor": k}, device_id_type=MESH,
        )

    for step in range(1, members):
        spread(lax.rem(j + step, members)).start()
    a_part[j] = a_loc[pl.ds(pl.multiple_of(j * part, 16), part), :]
    more.extend()
    more.relay()
    service(3, 0)
    for step in range(1, members):
        spread_from(lax.rem(j + step, members)).wait_recv()

    mine = pl.ds(pl.multiple_of(j * part, 16), part)
    group = span // a_part.shape[2]

    def lift(to, g):
        lane = pl.ds(g * a_part.shape[2], a_part.shape[2])
        return pltpu.make_async_remote_copy(
            src_ref=a_part.at[to * group + g], dst_ref=a_all.at[z, mine, lane], send_sem=xz_send.at[to, g],
            recv_sem=xz_recv.at[z, g], device_id={"dp": to}, device_id_type=MESH,
        )

    def lift_from(k, g):
        lane = pl.ds(g * a_part.shape[2], a_part.shape[2])
        view = a_all.at[k, mine, lane]
        return pltpu.make_async_remote_copy(
            src_ref=view, dst_ref=view, send_sem=xz_send.at[k, g], recv_sem=xz_recv.at[k, g],
            device_id={"dp": k}, device_id_type=MESH,
        )

    for step in range(1, planes):
        for g in range(group):
            lift(lax.rem(z + step, planes), g).start()
    for g in range(group):
        a_all[z, mine, pl.ds(g * a_part.shape[2], a_part.shape[2])] = a_part[z * group + g]
    more.share_near()
    more.share_far()
    for step in range(1, planes):
        for g in range(group):
            lift_from(lax.rem(z + step, planes), g).wait_recv()
    acts.begin()
    more.arrive(6, 7, 8, 9, 10)
    lax.fori_loop(1, chunks, project, 0)
    acts.relay()
    for n in range(1, chunks):
        service(1, n)
    acts.share_near()
    service(2, 1)
    acts.share_far()
    acts.arrive(6, 7, 8, 9, 10)
    for level in range(4, planes):
        service(level, 0)

    turn = 1 - 2 * (z // (planes // 2))

    def score(s, n):
        block = lax.rem(z + s * turn + planes, planes)
        at = pl.ds(pl.multiple_of(n * CHUNK, CHUNK), CHUNK)
        for q in range(queries):
            mixed = lax.dot_general(
                scaled[q], a_all[block, at, :], (((1,), (1,)), ((), ())), preferred_element_type=f32
            )
            csum[block, n, pl.ds(q, 1), :] = jnp.sum(mixed * g_all[block, n].astype(f32), axis=0, keepdims=True)

    def score_loop(lo, hi, n):
        def body(s, carry):
            score(s, n)
            return carry

        lax.fori_loop(lo, hi, body, 0)

    score_loop(0, planes, 0)
    for n in range(2, chunks):
        service(2, n)
    for n in range(1, chunks):
        score_loop(0, min(3, planes), n)
    for n in range(1, chunks):
        for level in range(3, planes):
            service(level, n)
        score_loop(min(3, planes), planes, n)

    per = res_ref.shape[1]
    lane_at = lax.broadcasted_iota(jnp.int32, (8, per), 1)
    each = CHUNK // seq_len
    for b in range(planes):
        tile = jnp.zeros((8, per), f32)
        for n in range(chunks):
            for h in range(each):
                total = jnp.sum(csum[b, n, :, h * seq_len:(h + 1) * seq_len], axis=1, keepdims=True)
                tile = tile + jnp.where(lane_at == n * each + h, total, 0.0)
        tiles[b] = tile

    def fold(to):
        return pltpu.make_async_remote_copy(
            src_ref=tiles.at[to], dst_ref=got_z.at[z], send_sem=rz_send.at[to], recv_sem=rz_recv.at[z],
            device_id={"dp": to}, device_id_type=MESH,
        )

    def fold_from(k):
        return pltpu.make_async_remote_copy(
            src_ref=got_z.at[k], dst_ref=got_z.at[k], send_sem=rz_send.at[k], recv_sem=rz_recv.at[k],
            device_id={"dp": k}, device_id_type=MESH,
        )

    for step in range(1, planes):
        fold(lax.rem(z + step, planes)).start()
    got_z[z] = tiles[z]
    for step in range(1, planes):
        fold_from(lax.rem(z + step, planes)).wait_recv()
    total = got_z[0]
    for b in range(1, planes):
        total = total + got_z[b]
    got_p[j] = total

    def share(to):
        return pltpu.make_async_remote_copy(
            src_ref=got_p.at[j], dst_ref=got_p.at[j], send_sem=rp_send.at[to], recv_sem=rp_recv.at[j],
            device_id={"tensor": to}, device_id_type=MESH,
        )

    def share_from(k):
        return pltpu.make_async_remote_copy(
            src_ref=got_p.at[k], dst_ref=got_p.at[k], send_sem=rp_send.at[k], recv_sem=rp_recv.at[k],
            device_id={"tensor": k}, device_id_type=MESH,
        )

    for step in range(1, members):
        share(lax.rem(j + step, members)).start()
    for step in range(1, members):
        share_from(lax.rem(j + step, members)).wait_recv()
    total = got_p[0]
    for k in range(1, members):
        total = total + got_p[k]
    res_ref[...] = total

    og.drain()
    more.drain()
    act.drain()
    acts.drain()
    for level in range(planes):
        for n in range(chunks):
            @pl.when((z - level >= 0) & (z < planes - 1))
            def _():
                up(z - level, n).wait_send()

            @pl.when((z + level < planes) & (z > 0))
            def _():
                down(z + level, n).wait_send()
    for step in range(1, members):
        to = lax.rem(j + step, members)
        spread(to).wait_send()
        share(to).wait_send()
    for step in range(1, planes):
        to = lax.rem(z + step, planes)
        for g in range(group):
            lift(to, g).wait_send()
        fold(to).wait_send()


def fits(planes, members, activations, out_grads_t, in_basis, query_proj, seq_count):
    rows, feats = activations.shape
    width, tokens = out_grads_t.shape
    cols, span = in_basis.shape[1], query_proj.shape[2]
    return (
        members == 8 and planes % 2 == 0 and rows == tokens and rows % (16 * members) == 0
        and feats % 128 == 0 and cols % 128 == 0 and span % cols == 0 and width % 16 == 0
        and tokens % CHUNK == 0 and tokens > CHUNK and width > 32 and CHUNK % (rows // seq_count) == 0 and (rows // seq_count) % 128 == 0
        and seq_count <= 128 and query_proj.shape[0] <= 8
    )


def local(planes, members, activations, out_grads_t, in_basis, out_basis_t, query_proj, eigvals, damping, lengths):
    seq_count = lengths.shape[0]
    if not fits(planes, members, activations, out_grads_t, in_basis, query_proj, seq_count):
        return generic(activations, out_grads_t, in_basis, out_basis_t, query_proj, eigvals, damping, lengths)
    bf16, f32 = jnp.bfloat16, jnp.float32
    rows, feats = activations.shape
    width, tokens = out_grads_t.shape
    features, cols = in_basis.shape
    depth = out_basis_t.shape[1]
    queries, _, span = query_proj.shape
    seq_len = rows // seq_count
    part, chunks, group = rows // members, tokens // CHUNK, span // cols
    position = lax.broadcasted_iota(jnp.int32, (seq_count, seq_len), 1)
    keep = jnp.broadcast_to((position < lengths[:, None]).astype(f32).reshape(1, tokens), (8, tokens))
    any_space = pl.BlockSpec(memory_space=pl.ANY)
    vmem = pl.BlockSpec(memory_space=pltpu.VMEM)
    dma = pltpu.SemaphoreType.DMA
    res = pl.pallas_call(
        functools.partial(kernel, planes, seq_len),
        out_shape=jax.ShapeDtypeStruct((8, 128), f32),
        in_specs=[any_space] * 6 + [vmem, pl.BlockSpec(memory_space=pltpu.SMEM)],
        out_specs=vmem,
        scratch_shapes=[
            pltpu.VMEM((members * width, tokens), bf16),
            pltpu.VMEM((members, rows, feats), bf16),
            pltpu.VMEM((features, cols), bf16),
            pltpu.VMEM((width, depth), bf16),
            pltpu.VMEM((queries, width, span), bf16),
            pltpu.VMEM((width, span), f32),
            pltpu.VMEM((planes, rows, span), bf16),
            pltpu.VMEM((members, part, cols), bf16),
            pltpu.VMEM((rows, cols), bf16),
            pltpu.VMEM((rows, cols), f32),
            pltpu.VMEM((planes, chunks, width, CHUNK), bf16),
            pltpu.VMEM((width, CHUNK), f32),
            pltpu.VMEM((planes, chunks, 8, CHUNK), f32),
            pltpu.VMEM((planes, 8, 128), f32),
            pltpu.VMEM((planes, 8, 128), f32),
            pltpu.VMEM((members, 8, 128), f32),
            dma((6,)), dma((4, 11)), dma((4, 11)),
            dma((planes, chunks)), dma((planes, chunks)), dma((planes, chunks)), dma((planes, chunks)),
            dma((members,)), dma((members,)), dma((planes, group)), dma((planes, group)),
            dma((planes,)), dma((planes,)), dma((members,)), dma((members,)),
        ],
        compiler_params=pltpu.CompilerParams(
            collective_id=0, has_side_effects=True, vmem_limit_bytes=63 * 1024 * 1024
        ),
    )(activations, out_grads_t, in_basis, out_basis_t, query_proj, eigvals, keep, damping)
    norm_factor = (features * depth * seq_len) ** (-0.5)
    return res[:queries, :seq_count].T * norm_factor


def solution(mesh):
    placed = (
        P("dp", "tensor"),
        P("tensor", "dp"),
        P(None, "tensor"),
        P("tensor", None),
        P(None, "tensor", "dp"),
        P("tensor", "dp"),
        P(),
        P("dp"),
    )
    return jax.shard_map(
        functools.partial(local, mesh.shape["dp"], mesh.shape["tensor"]), mesh=mesh, in_specs=placed, out_specs=P("dp", None), check_vma=False
    )
```

profile of v0, /device:TPU:0, one launch (start us, length us, event | category | flops | bytes accessed | tf_op | source)
XLA Modules:
  0.0 141.7 jit_solution(4030502715255078676)
XLA Ops:
  0.7 0.7 convert_bitcast_fusion
  1.4 0.6 broadcast_in_dim.2.keep_ref
  2.0 138.5 %shard_map.82 = f32[8,128]{1,0:T(8,128)} custom-call(bf16[768,512]{1,0:T(8,128)(2,1)} %act_ref.1, bf16[688,768]{1,0:T(8,128)(2,1)} %og_ref.1, bf16[4096,512]{1,0:T(8,128)(2,1)} %in_ref.1, bf16[688,5504]{1,0:T(8,128)(2,1)} %out_ref.1, bf16[4,688,1024]{2,1,0:T(8,128)(2,1)} %query_ref.1, f32[688,1024]{1,0:T(8,128)} %eig_ref.1, ...), custom_call_target="tpu_custom_call" | custom-call | tf_op jit(solution)/shard_map/pallas_call | solution.py:502
  140.5 1.3 multiply_bitcast_fusion
where the time goes:
time: 142 us
  Pallas kernels  138 us (97%)
  other arithmetic  1.98 us (1%)
    pallas_call x1, Pallas kernels, local(): pl.pallas_call(functools.partial(kernel, planes, seq_len), out_shape=jax....  138 us

commit v1 on v0

v1 whole, which is shorter than its diff:
```python
import functools

import jax
import jax.numpy as jnp
from jax import lax
from jax.experimental import pallas as pl
from jax.experimental.pallas import tpu as pltpu
from jax.sharding import PartitionSpec as P


def generic(activations, out_grads_t, in_basis, out_basis_t, query_proj, eigvals, damping, lengths):
    bf16, f32 = jnp.bfloat16, jnp.float32
    seq_count = lengths.shape[0]
    full_act = lax.all_gather(activations, "tensor", axis=1, tiled=True)
    token_rows = full_act.shape[0]
    seq_len = token_rows // seq_count
    act_local = jnp.dot(full_act, in_basis, preferred_element_type=f32).astype(bf16)
    act_full = lax.all_gather(act_local, "tensor", axis=1, tiled=True)
    features = act_full.shape[1]
    act_proj = lax.all_to_all(act_full, "dp", split_axis=1, concat_axis=0, tiled=True)
    grad_full = jnp.dot(
        out_basis_t, lax.all_gather(out_grads_t, "tensor", axis=0, tiled=True), preferred_element_type=f32
    )
    position = lax.broadcasted_iota(jnp.int32, (seq_count, seq_len), 1)
    keep = (position < lengths[:, None]).astype(f32).reshape(1, token_rows)
    grad_local = (grad_full * keep).astype(bf16)
    grad_proj = lax.all_gather(grad_local, "dp", axis=1, tiled=True)
    scaled = (query_proj.astype(f32) / (eigvals + damping[0])).astype(bf16)
    mixed = jnp.einsum("td,qjd->qjt", act_proj, scaled, preferred_element_type=f32)
    weighted = mixed * grad_proj.astype(f32)[None, :, :]
    query_count, width, tokens = weighted.shape
    partial_value = jnp.sum(weighted.reshape(query_count, width, tokens // seq_len, seq_len), axis=(1, 3)).T
    totals = lax.psum(partial_value, ("dp", "tensor"))
    mine = lax.dynamic_slice_in_dim(totals, lax.axis_index("dp") * seq_count, seq_count, 0)
    norm_factor = (features * out_basis_t.shape[1] * seq_len) ** (-0.5)
    return mine * norm_factor


MESH = pl.DeviceIdType.MESH


def kernel(
    act_ref, og_ref, in_ref, out_ref, query_ref, eig_ref, len_ref, damp_ref, res_ref,
    og_all, act_all, in_b, out_b, scaled, eig, a_all, a_part, a_loc, a_acc, g_all, g_acc, csum, tiles, got_z, got_p,
    load_sem, gs_send, gs_recv, up_send, up_recv, dn_send, dn_recv, xp_send, xp_recv, xz_send, xz_recv,
    rz_send, rz_recv, rp_send, rp_recv,
):
    bf16, f32 = jnp.bfloat16, jnp.float32
    z, j = lax.axis_index("dp"), lax.axis_index("tensor")
    members, rows, feats = act_all.shape
    planes, units, width, unit = g_all.shape
    depth = out_b.shape[1]
    queries, span = scaled.shape[0], scaled.shape[2]
    cols = a_loc.shape[2]
    part = unit // members
    pairs = units // 2
    group = span // cols
    half_planes = planes // 2
    pieces = [(0, 1), (1, 1)] + [(2 * n, 2) for n in range(1, pairs)]
    jx = j + 2 - 4 * lax.rem(j // 2, 2)
    jy = j + 4 - 8 * (j // 4)
    jd = jx + 4 - 8 * (j // 4)

    def mate(k):
        return k + 1 - 2 * lax.rem(k, 2)

    jp = mate(j)

    loads = [
        pltpu.make_async_copy(og_ref, og_all.at[pl.ds(pl.multiple_of(j * width, 16), width), :], load_sem.at[0]),
        pltpu.make_async_copy(act_ref, act_all.at[j], load_sem.at[1]),
        pltpu.make_async_copy(query_ref, scaled, load_sem.at[2]),
        pltpu.make_async_copy(eig_ref, eig, load_sem.at[3]),
        pltpu.make_async_copy(out_ref, out_b, load_sem.at[4]),
        pltpu.make_async_copy(in_ref, in_b, load_sem.at[5]),
    ]
    for load in loads:
        load.start()

    barrier = pltpu.get_barrier_semaphore()
    for step in range(1, members):
        pl.semaphore_signal(barrier, inc=1, device_id={"tensor": lax.rem(j + step, members)}, device_id_type=MESH)
    for step in range(1, planes):
        pl.semaphore_signal(barrier, inc=1, device_id={"dp": lax.rem(z + step, planes)}, device_id_type=MESH)

    def meet():
        pl.semaphore_wait(barrier, members + planes - 2)

    class Gather:
        def __init__(self, op, view, own):
            self.op, self.view, self.own = op, view, own
            self.plan = [
                (j, 0, jx), (j, 1, jx), (jy, 1, jx),
                (j, 1, jy), (j, 0, jy), (jx, 0, jy),
                (j, None, jp), (jx, None, jp), (jy, None, jp), (jd, 0, jp), (jd, 1, jp),
            ]
            self.landed = [
                (jx, 0), (jx, 1), (jd, 1),
                (jy, 1), (jy, 0), (jd, 0),
                (jp, None), (mate(jx), None), (mate(jy), None), (mate(jd), 0), (mate(jd), 1),
            ]

        def copy(self, slot):
            block, half, target = self.plan[slot]
            src = self.own(half) if slot in (0, 1, 3, 4, 6) else self.view(block, half)
            return pltpu.make_async_remote_copy(
                src_ref=src, dst_ref=self.view(block, half), send_sem=gs_send.at[self.op, slot],
                recv_sem=gs_recv.at[self.op, slot], device_id={"tensor": target}, device_id_type=MESH,
            )

        def start(self, *slots):
            for slot in slots:
                self.copy(slot).start()

        def arrive(self, *slots):
            for slot in slots:
                block, half = self.landed[slot]
                view = self.view(block, half)
                pltpu.make_async_remote_copy(
                    src_ref=view, dst_ref=view, send_sem=gs_send.at[self.op, slot],
                    recv_sem=gs_recv.at[self.op, slot], device_id={"tensor": jp}, device_id_type=MESH,
                ).wait_recv()

        def begin(self):
            self.start(0, 3, 1, 4, 6)

        def relay(self):
            self.arrive(0)
            self.start(5)
            self.arrive(3)
            self.start(2)

        def near(self):
            self.arrive(1)
            self.start(7)
            self.arrive(4)
            self.start(8)

        def far(self):
            self.arrive(5)
            self.start(9)
            self.arrive(2)
            self.start(10)

        def finish(self):
            self.arrive(6, 7, 8, 9, 10)

        def drain(self):
            for slot in range(len(self.plan)):
                self.copy(slot).wait_send()

    cut = (width // 2 + 15) // 16 * 16

    def og_rows(h):
        return (0, width) if h is None else ((0, cut), (cut, width - cut))[h]

    def og_gather(op, first, count):
        lanes = pl.ds(first * unit, count * unit)

        def view(k, h):
            top, size = og_rows(h)
            return og_all.at[pl.ds(pl.multiple_of(k * width + top, 16), size), lanes]

        return Gather(op, view, lambda h: og_ref.at[pl.ds(*og_rows(h)), lanes])

    def act_gather(op, r):
        def at(h):
            size = 2 * unit if h is None else unit
            return pl.ds(2 * unit * r + unit * (h or 0), size)

        return Gather(op, lambda k, h: act_all.at[k, at(h), :], lambda h: act_ref.at[at(h), :])

    def acts_gather(op, u):
        def view(k, h):
            at = pl.ds(pl.multiple_of(k * part, 16), part)
            if h is None:
                return a_all.at[u, :, at, :]
            return a_all.at[u, pl.ds(h * half_planes, half_planes), at, :]

        return Gather(op, view, lambda h: view(j, h))

    og = [og_gather(n, *piece) for n, piece in enumerate(pieces)]
    act = [act_gather(len(og) + r, r) for r in range(pairs)]
    acts = [acts_gather(len(og) + len(act) + u, u) for u in range(units)]

    def scale_all():
        csum[...] = jnp.zeros_like(csum)
        loads[2].wait()
        loads[3].wait()
        step_rows = 16

        def scale(i, carry):
            at = pl.ds(pl.multiple_of(i * step_rows, step_rows), step_rows)
            below = eig[at, :] + damp_ref[0]
            for q in range(queries):
                scaled[q, at, :] = (scaled[q, at, :].astype(f32) / below).astype(bf16)
            return carry

        lax.fori_loop(0, width // step_rows, scale, 0)

    def chain(n, block, sends, recvs, to):
        first, count = pieces[n]
        view = g_all.at[block, pl.ds(first, count)]
        return pltpu.make_async_remote_copy(
            src_ref=view, dst_ref=view, send_sem=sends.at[block, n], recv_sem=recvs.at[block, n],
            device_id={"dp": to}, device_id_type=MESH,
        )

    def up(block, n):
        return chain(n, block, up_send, up_recv, lax.rem(z + 1, planes))

    def down(block, n):
        return chain(n, block, dn_send, dn_recv, lax.rem(z + planes - 1, planes))

    def service(level, n):
        @pl.when(z - level >= 0)
        def _():
            up(z - level, n).wait_recv()

        @pl.when((z - level >= 0) & (z < planes - 1))
        def _():
            up(z - level, n).start()

        @pl.when(z + level < planes)
        def _():
            down(z + level, n).wait_recv()

        @pl.when((z + level < planes) & (z > 0))
        def _():
            down(z + level, n).start()

    k_tile = 6 * unit
    k_full = depth // k_tile

    def project(n):
        first, count = pieces[n]
        wide = count * unit
        at, to = pl.ds(first * unit, wide), pl.ds(0, wide)
        k_rest = depth - k_full * k_tile
        if k_rest:
            g_acc[:, to] = jnp.dot(
                out_b[:, pl.ds(k_full * k_tile, k_rest)], og_all[pl.ds(k_full * k_tile, k_rest), at],
                preferred_element_type=f32,
            )
        else:
            g_acc[:, to] = jnp.zeros((width, wide), f32)

        def inner(k, c):
            deep = pl.ds(pl.multiple_of(k * k_tile, k_tile), k_tile)
            g_acc[:, to] += jnp.dot(out_b[:, deep], og_all[deep, at], preferred_element_type=f32)
            return c

        lax.fori_loop(0, k_full, inner, 0)
        lane = lax.broadcasted_iota(jnp.int32, (1, unit), 1)
        for i in range(count):
            keep = (lane < len_ref[first + i]).astype(f32)
            g_all[z, first + i] = (g_acc[:, pl.ds(i * unit, unit)] * keep).astype(bf16)

        @pl.when(z < planes - 1)
        def _():
            up(z, n).start()

        @pl.when(z > 0)
        def _():
            down(z, n).start()

    def contract(r):
        at = pl.ds(2 * unit * r, 2 * unit)
        a_acc[...] = jnp.zeros_like(a_acc)

        def body(k, carry):
            deep = pl.ds(pl.multiple_of(k * feats, feats), feats)
            a_acc[...] += jnp.dot(act_all[k, at, :], in_b[deep, :], preferred_element_type=f32)
            return carry

        lax.fori_loop(0, members, body, 0)
        for s in range(2):
            a_loc[2 * r + s] = a_acc[pl.ds(s * unit, unit), :].astype(bf16)

    def own_rows(k):
        return pl.ds(pl.multiple_of(k * part, 16), part)

    def spread_to(r, to):
        return pltpu.make_async_remote_copy(
            src_ref=a_loc.at[pl.ds(2 * r, 2), own_rows(to), :],
            dst_ref=a_part.at[r, j], send_sem=xp_send.at[r, to], recv_sem=xp_recv.at[r, j],
            device_id={"tensor": to}, device_id_type=MESH,
        )

    def spread_from(r, k):
        return pltpu.make_async_remote_copy(
            src_ref=a_part.at[r, k], dst_ref=a_part.at[r, k], send_sem=xp_send.at[r, k], recv_sem=xp_recv.at[r, k],
            device_id={"tensor": k}, device_id_type=MESH,
        )

    def spread(r):
        for step in range(1, members):
            spread_to(r, lax.rem(j + step, members)).start()
        a_part[r, j] = a_loc[pl.ds(2 * r, 2), own_rows(j), :]

    def lift_to(r, to, g):
        lane = pl.ds(g * cols, cols)
        return pltpu.make_async_remote_copy(
            src_ref=a_part.at[r, to * group + g], dst_ref=a_all.at[pl.ds(2 * r, 2), z, own_rows(j), lane],
            send_sem=xz_send.at[r, to, g], recv_sem=xz_recv.at[r, z, g], device_id={"dp": to}, device_id_type=MESH,
        )

    def lift_from(r, k, g):
        lane = pl.ds(g * cols, cols)
        view = a_all.at[pl.ds(2 * r, 2), k, own_rows(j), lane]
        return pltpu.make_async_remote_copy(
            src_ref=view, dst_ref=view, send_sem=xz_send.at[r, k, g], recv_sem=xz_recv.at[r, k, g],
            device_id={"dp": k}, device_id_type=MESH,
        )

    def lift(r):
        for step in range(1, members):
            spread_from(r, lax.rem(j + step, members)).wait_recv()
        for step in range(1, planes):
            for g in range(group):
                lift_to(r, lax.rem(z + step, planes), g).start()
        for g in range(group):
            a_all[pl.ds(2 * r, 2), z, own_rows(j), pl.ds(g * cols, cols)] = a_part[r, z * group + g]

    def lifted(r):
        for step in range(1, planes):
            for g in range(group):
                lift_from(r, lax.rem(z + step, planes), g).wait_recv()

    def score(u):
        def body(h, carry):
            block = a_all[u, pl.ds(2 * h, 2)].reshape(2 * unit, span)
            for q in range(queries):
                mixed = lax.dot_general(
                    scaled[q], block, (((1,), (1,)), ((), ())), preferred_element_type=f32
                )
                for b in range(2):
                    csum[2 * h + b, u, pl.ds(q, 1), :] = jnp.sum(
                        mixed[:, b * unit:(b + 1) * unit] * g_all[2 * h + b, u].astype(f32), axis=0, keepdims=True
                    )
            return carry

        lax.fori_loop(0, half_planes, body, 0)

    def loaded(*which):
        for n in which:
            loads[n].wait()

    meet()
    og[0].begin()
    scale_all()
    og[0].relay()
    og[1].begin()
    og[0].near()
    og[0].far()
    og[0].finish()
    loaded(0, 4)
    project(0)
    og[1].relay()
    og[2].begin()
    og[1].near()
    og[1].far()
    og[1].finish()
    project(1)
    og[2].relay()
    act[0].begin()
    og[2].near()
    service(1, 0)
    og[2].far()
    og[2].finish()
    project(2)
    service(2, 0)
    act[0].relay()
    act[1].begin()
    act[0].near()
    service(1, 1)
    act[0].far()
    act[0].finish()
    loaded(1, 5)
    contract(0)
    spread(0)
    act[1].relay()
    og[3].begin()
    service(3, 0)
    act[1].near()
    service(2, 1)
    act[1].far()
    act[1].finish()
    contract(1)
    spread(1)
    lift(0)
    og[3].relay()
    act[2].begin()
    service(1, 2)
    og[3].near()
    service(3, 1)
    og[3].far()
    og[3].finish()
    project(3)
    lift(1)
    act[2].relay()
    lifted(0)
    acts[0].begin()
    act[2].near()
    service(2, 2)
    act[2].far()
    act[2].finish()
    contract(2)
    spread(2)
    acts[0].relay()
    acts[1].begin()
    acts[0].near()
    acts[0].far()
    acts[0].finish()
    lift(2)
    service(3, 2)
    score(0)
    service(1, 3)
    acts[1].relay()
    lifted(1)
    acts[2].begin()
    acts[1].near()
    acts[1].far()
    acts[1].finish()
    service(2, 3)
    score(1)
    acts[2].relay()
    acts[3].begin()
    acts[2].near()
    acts[2].far()
    acts[2].finish()
    score(2)
    acts[3].relay()
    lifted(2)
    acts[4].begin()
    acts[3].near()
    acts[3].far()
    acts[3].finish()
    score(3)
    acts[4].relay()
    acts[5].begin()
    acts[4].near()
    acts[4].far()
    acts[4].finish()
    service(3, 3)
    score(4)
    acts[5].relay()
    acts[5].near()
    acts[5].far()
    acts[5].finish()
    score(5)
    per = res_ref.shape[1]
    lane_at = lax.broadcasted_iota(jnp.int32, (8, per), 1)
    for b in range(planes):
        tile = jnp.zeros((8, per), f32)
        for u in range(units):
            total = jnp.sum(csum[b, u], axis=1, keepdims=True)
            tile = tile + jnp.where(lane_at == u, total, 0.0)
        tiles[b] = tile

    def fold(to):
        return pltpu.make_async_remote_copy(
            src_ref=tiles.at[to], dst_ref=got_z.at[z], send_sem=rz_send.at[to], recv_sem=rz_recv.at[z],
            device_id={"dp": to}, device_id_type=MESH,
        )

    def fold_from(k):
        return pltpu.make_async_remote_copy(
            src_ref=got_z.at[k], dst_ref=got_z.at[k], send_sem=rz_send.at[k], recv_sem=rz_recv.at[k],
            device_id={"dp": k}, device_id_type=MESH,
        )

    def fold_all():
        for step in range(1, planes):
            fold(lax.rem(z + step, planes)).start()
        got_z[z] = tiles[z]
        for step in range(1, planes):
            fold_from(lax.rem(z + step, planes)).wait_recv()
        total = got_z[0]
        for b in range(1, planes):
            total = total + got_z[b]
        got_p[j] = total

    def share(to):
        return pltpu.make_async_remote_copy(
            src_ref=got_p.at[j], dst_ref=got_p.at[j], send_sem=rp_send.at[to], recv_sem=rp_recv.at[j],
            device_id={"tensor": to}, device_id_type=MESH,
        )

    def share_from(k):
        return pltpu.make_async_remote_copy(
            src_ref=got_p.at[k], dst_ref=got_p.at[k], send_sem=rp_send.at[k], recv_sem=rp_recv.at[k],
            device_id={"tensor": k}, device_id_type=MESH,
        )

    def share_all():
        for step in range(1, members):
            share(lax.rem(j + step, members)).start()
        for step in range(1, members):
            share_from(lax.rem(j + step, members)).wait_recv()
        total = got_p[0]
        for k in range(1, members):
            total = total + got_p[k]
        res_ref[...] = total

    def drain_all():
        for op in og + act + acts:
            op.drain()
        for level in range(planes):
            for n in range(len(pieces)):
                @pl.when((z - level >= 0) & (z < planes - 1))
                def _():
                    up(z - level, n).wait_send()

                @pl.when((z + level < planes) & (z > 0))
                def _():
                    down(z + level, n).wait_send()
        for step in range(1, members):
            to = lax.rem(j + step, members)
            for r in range(pairs):
                spread_to(r, to).wait_send()
            share(to).wait_send()
        for step in range(1, planes):
            to = lax.rem(z + step, planes)
            for r in range(pairs):
                for g in range(group):
                    lift_to(r, to, g).wait_send()
            fold(to).wait_send()

    fold_all()
    share_all()
    drain_all()


def fits(planes, members, activations, out_grads_t, in_basis, query_proj, seq_count):
    rows, feats = activations.shape
    width, tokens = out_grads_t.shape
    cols, span = in_basis.shape[1], query_proj.shape[2]
    unit = rows // seq_count
    return (
        members == 8 and planes == 4 and rows == tokens and rows == unit * seq_count and unit == 16 * members
        and seq_count == 6 and feats % 128 == 0 and cols % 128 == 0 and span % cols == 0 and span == 2 * cols
        and width % 16 == 0 and width > 32 and query_proj.shape[0] <= 8
    )


def local(planes, members, activations, out_grads_t, in_basis, out_basis_t, query_proj, eigvals, damping, lengths):
    seq_count = lengths.shape[0]
    if not fits(planes, members, activations, out_grads_t, in_basis, query_proj, seq_count):
        return generic(activations, out_grads_t, in_basis, out_basis_t, query_proj, eigvals, damping, lengths)
    bf16, f32 = jnp.bfloat16, jnp.float32
    rows, feats = activations.shape
    width, tokens = out_grads_t.shape
    features, cols = in_basis.shape
    depth = out_basis_t.shape[1]
    queries, _, span = query_proj.shape
    unit = rows // seq_count
    part, pairs, group = unit // members, seq_count // 2, span // cols
    pieces = pairs + 1
    ops = pieces + pairs + seq_count
    any_space = pl.BlockSpec(memory_space=pl.ANY)
    vmem = pl.BlockSpec(memory_space=pltpu.VMEM)
    smem = pl.BlockSpec(memory_space=pltpu.SMEM)
    dma = pltpu.SemaphoreType.DMA
    res = pl.pallas_call(
        kernel,
        out_shape=jax.ShapeDtypeStruct((8, 128), f32),
        in_specs=[any_space] * 6 + [smem, smem],
        out_specs=vmem,
        scratch_shapes=[
            pltpu.VMEM((members * width, tokens), bf16),
            pltpu.VMEM((members, rows, feats), bf16),
            pltpu.VMEM((features, cols), bf16),
            pltpu.VMEM((width, depth), bf16),
            pltpu.VMEM((queries, width, span), bf16),
            pltpu.VMEM((width, span), f32),
            pltpu.VMEM((seq_count, planes, unit, span), bf16),
            pltpu.VMEM((pairs, members, 2, part, cols), bf16),
            pltpu.VMEM((seq_count, unit, cols), bf16),
            pltpu.VMEM((2 * unit, cols), f32),
            pltpu.VMEM((planes, seq_count, width, unit), bf16),
            pltpu.VMEM((width, 2 * unit), f32),
            pltpu.VMEM((planes, seq_count, 8, unit), f32),
            pltpu.VMEM((planes, 8, 128), f32),
            pltpu.VMEM((planes, 8, 128), f32),
            pltpu.VMEM((members, 8, 128), f32),
            dma((6,)), dma((ops, 11)), dma((ops, 11)),
            dma((planes, pieces)), dma((planes, pieces)), dma((planes, pieces)), dma((planes, pieces)),
            dma((pairs, members)), dma((pairs, members)), dma((pairs, planes, group)), dma((pairs, planes, group)),
            dma((planes,)), dma((planes,)), dma((members,)), dma((members,)),
        ],
        compiler_params=pltpu.CompilerParams(
            collective_id=0, has_side_effects=True, vmem_limit_bytes=63 * 1024 * 1024
        ),
    )(activations, out_grads_t, in_basis, out_basis_t, query_proj, eigvals, lengths, damping)
    norm_factor = (features * depth * unit) ** (-0.5)
    return res[:queries, :seq_count].T * norm_factor


def solution(mesh):
    placed = (
        P("dp", "tensor"),
        P("tensor", "dp"),
        P(None, "tensor"),
        P("tensor", None),
        P(None, "tensor", "dp"),
        P("tensor", "dp"),
        P(),
        P("dp"),
    )
    return jax.shard_map(
        functools.partial(local, mesh.shape["dp"], mesh.shape["tensor"]), mesh=mesh, in_specs=placed, out_specs=P("dp", None), check_vma=False
    )
```

time: 142 us -> 155 us (1.092)
  Pallas kernels: 138 us -> 153 us
    pallas_call x1, Pallas kernels: 138 us -> 153 us  [local(): pl.pallas_call(kernel, out_shape=jax.ShapeDtypeStruct((8, 128), f32), in_...]
where the time goes in v1:
time: 155 us
  Pallas kernels  153 us (99%)
    pallas_call x1, Pallas kernels, local(): pl.pallas_call(kernel, out_shape=jax.ShapeDtypeStruct((8, 128), f32), in_...  153 us

profile of v1, /device:TPU:0, one launch (start us, length us, event | category | flops | bytes accessed | tf_op | source)
XLA Modules:
  0.0 154.9 jit_solution(4323563047299461163)
XLA Ops:
  0.7 152.9 %shard_map.82 = f32[8,128]{1,0:T(8,128)} custom-call(bf16[768,512]{1,0:T(8,128)(2,1)} %act_ref.1, bf16[688,768]{1,0:T(8,128)(2,1)} %og_ref.1, bf16[4096,512]{1,0:T(8,128)(2,1)} %in_ref.1, bf16[688,5504]{1,0:T(8,128)(2,1)} %out_ref.1, bf16[4,688,1024]{2,1,0:T(8,128)(2,1)} %query_ref.1, f32[688,1024]{1,0:T(8,128)} %eig_ref.1, s32[6]{0:T(128)} %len_ref.1, ...), custom_call_target="tpu_custom_call" | custom-call | tf_op jit(solution)/shard_map/pallas_call | solution.py:565
  153.6 1.3 multiply_bitcast_fusion

commit v2 on v1

--- a/solution.py
+++ b/solution.py
@@ -87,67 +87,68 @@
         pl.semaphore_wait(barrier, members + planes - 2)
 
     class Gather:
-        def __init__(self, op, view, own):
-            self.op, self.view, self.own = op, view, own
+        def __init__(self, op, view, own, several):
+            self.op, self.view, self.own, self.several = op, view, own, several
             self.plan = [
                 (j, 0, jx), (j, 1, jx), (jy, 1, jx),
                 (j, 1, jy), (j, 0, jy), (jx, 0, jy),
                 (j, None, jp), (jx, None, jp), (jy, None, jp), (jd, 0, jp), (jd, 1, jp),
             ]
-            self.landed = [
-                (jx, 0), (jx, 1), (jd, 1),
-                (jy, 1), (jy, 0), (jd, 0),
-                (jp, None), (mate(jx), None), (mate(jy), None), (mate(jd), 0), (mate(jd), 1),
-            ]
+            self.lane = (0, 2, 3, 1, 2, 3, 4, 4, 4, 5, 5)
 
         def copy(self, slot):
             block, half, target = self.plan[slot]
             src = self.own(half) if slot in (0, 1, 3, 4, 6) else self.view(block, half)
             return pltpu.make_async_remote_copy(
-                src_ref=src, dst_ref=self.view(block, half), send_sem=gs_send.at[self.op, slot],
-                recv_sem=gs_recv.at[self.op, slot], device_id={"tensor": target}, device_id_type=MESH,
+                src_ref=src, dst_ref=self.view(block, half), send_sem=gs_send.at[self.op],
+                recv_sem=gs_recv.at[self.op, self.lane[slot]], device_id={"tensor": target}, device_id_type=MESH,
             )
 
         def start(self, *slots):
             for slot in slots:
                 self.copy(slot).start()
 
-        def arrive(self, *slots):
-            for slot in slots:
-                block, half = self.landed[slot]
-                view = self.view(block, half)
-                pltpu.make_async_remote_copy(
-                    src_ref=view, dst_ref=view, send_sem=gs_send.at[self.op, slot],
-                    recv_sem=gs_recv.at[self.op, slot], device_id={"tensor": jp}, device_id_type=MESH,
-                ).wait_recv()
+        def arrive(self, lane, view):
+            pltpu.make_async_remote_copy(
+                src_ref=view, dst_ref=view, send_sem=gs_send.at[self.op],
+                recv_sem=gs_recv.at[self.op, lane], device_id={"tensor": jp}, device_id_type=MESH,
+            ).wait_recv()
 
         def begin(self):
             self.start(0, 3, 1, 4, 6)
 
+        def open(self):
+            self.start(0, 3)
+
+        def extend(self):
+            self.start(1, 4, 6)
+
         def relay(self):
-            self.arrive(0)
+            self.arrive(0, self.view(jx, 0))
             self.start(5)
-            self.arrive(3)
+            self.arrive(1, self.view(jy, 1))
             self.start(2)
 
         def near(self):
-            self.arrive(1)
-            self.start(7)
-            self.arrive(4)
-            self.start(8)
+            self.arrive(2, self.view(jx, None))
+            self.start(7, 8)
 
         def far(self):
-            self.arrive(5)
-            self.start(9)
-            self.arrive(2)
-            self.start(10)
+            self.arrive(3, self.view(jd, None))
+            self.start(9, 10)
+
+        def paired(self):
+            self.arrive(4, self.several(3))
 
         def finish(self):
-            self.arrive(6, 7, 8, 9, 10)
+            self.arrive(5, self.view(mate(jd), None))
 
         def drain(self):
-            for slot in range(len(self.plan)):
-                self.copy(slot).wait_send()
+            view = self.several(len(self.plan) - 4)
+            pltpu.make_async_remote_copy(
+                src_ref=view, dst_ref=view, send_sem=gs_send.at[self.op],
+                recv_sem=gs_recv.at[self.op, 0], device_id={"tensor": jp}, device_id_type=MESH,
+            ).wait_send()
 
     cut = (width // 2 + 15) // 16 * 16
 
@@ -161,14 +162,20 @@
             top, size = og_rows(h)
             return og_all.at[pl.ds(pl.multiple_of(k * width + top, 16), size), lanes]
 
-        return Gather(op, view, lambda h: og_ref.at[pl.ds(*og_rows(h)), lanes])
+        return Gather(
+            op, view, lambda h: og_ref.at[pl.ds(*og_rows(h)), lanes],
+            lambda count: og_all.at[pl.ds(0, count * width), lanes],
+        )
 
     def act_gather(op, r):
         def at(h):
             size = 2 * unit if h is None else unit
             return pl.ds(2 * unit * r + unit * (h or 0), size)
 
-        return Gather(op, lambda k, h: act_all.at[k, at(h), :], lambda h: act_ref.at[at(h), :])
+        return Gather(
+            op, lambda k, h: act_all.at[k, at(h), :], lambda h: act_ref.at[at(h), :],
+            lambda count: act_all.at[pl.ds(0, count), at(None), :],
+        )
 
     def acts_gather(op, u):
         def view(k, h):
@@ -177,7 +184,7 @@
                 return a_all.at[u, :, at, :]
             return a_all.at[u, pl.ds(h * half_planes, half_planes), at, :]
 
-        return Gather(op, view, lambda h: view(j, h))
+        return Gather(op, view, lambda h: view(j, h), lambda count: a_all.at[u, :, pl.ds(0, count * part), :])
 
     og = [og_gather(n, *piece) for n, piece in enumerate(pieces)]
     act = [act_gather(len(og) + r, r) for r in range(pairs)]
@@ -202,8 +209,14 @@
         first, count = pieces[n]
         view = g_all.at[block, pl.ds(first, count)]
         return pltpu.make_async_remote_copy(
-            src_ref=view, dst_ref=view, send_sem=sends.at[block, n], recv_sem=recvs.at[block, n],
+            src_ref=view, dst_ref=view, send_sem=sends.at[block], recv_sem=recvs.at[block, n],
             device_id={"dp": to}, device_id_type=MESH,
+        )
+
+    def whole(block, sends, recvs):
+        return pltpu.make_async_remote_copy(
+            src_ref=g_all.at[block], dst_ref=g_all.at[block], send_sem=sends.at[block], recv_sem=recvs.at[block, 0],
+            device_id={"dp": lax.rem(z + 1, planes)}, device_id_type=MESH,
         )
 
     def up(block, n):
@@ -231,6 +244,26 @@
 
     k_tile = 6 * unit
     k_full = depth // k_tile
+
+    k_half = members // 2 * width
+    k_near, k_next = k_half // k_tile, -(-k_half // k_tile)
+    upper = j // (members // 2)
+
+    def deepen(n, lo, hi, offset):
+        first, count = pieces[n]
+        at, to = pl.ds(first * unit, count * unit), pl.ds(0, count * unit)
+
+        def inner(k, c):
+            deep = pl.ds(pl.multiple_of((k + offset) * k_tile, k_tile), k_tile)
+            g_acc[:, to] += jnp.dot(out_b[:, deep], og_all[deep, at], preferred_element_type=f32)
+            return c
+
+        lax.fori_loop(lo, hi, inner, 0)
+
+    def project_near(n):
+        wide = pieces[n][1] * unit
+        g_acc[:, pl.ds(0, wide)] = jnp.zeros((width, wide), f32)
+        deepen(n, 0, k_near, upper * k_next)
 
     def project(n):
         first, count = pieces[n]
@@ -238,19 +271,11 @@
         at, to = pl.ds(first * unit, wide), pl.ds(0, wide)
         k_rest = depth - k_full * k_tile
         if k_rest:
-            g_acc[:, to] = jnp.dot(
+            g_acc[:, to] += jnp.dot(
                 out_b[:, pl.ds(k_full * k_tile, k_rest)], og_all[pl.ds(k_full * k_tile, k_rest), at],
                 preferred_element_type=f32,
             )
-        else:
-            g_acc[:, to] = jnp.zeros((width, wide), f32)
-
-        def inner(k, c):
-            deep = pl.ds(pl.multiple_of(k * k_tile, k_tile), k_tile)
-            g_acc[:, to] += jnp.dot(out_b[:, deep], og_all[deep, at], preferred_element_type=f32)
-            return c
-
-        lax.fori_loop(0, k_full, inner, 0)
+        deepen(n, 0, k_full - k_near, (1 - upper) * k_near)
         lane = lax.broadcasted_iota(jnp.int32, (1, unit), 1)
         for i in range(count):
             keep = (lane < len_ref[first + i]).astype(f32)
@@ -283,14 +308,15 @@
     def spread_to(r, to):
         return pltpu.make_async_remote_copy(
             src_ref=a_loc.at[pl.ds(2 * r, 2), own_rows(to), :],
-            dst_ref=a_part.at[r, j], send_sem=xp_send.at[r, to], recv_sem=xp_recv.at[r, j],
+            dst_ref=a_part.at[r, j], send_sem=xp_send.at[r], recv_sem=xp_recv.at[r],
             device_id={"tensor": to}, device_id_type=MESH,
         )
 
-    def spread_from(r, k):
-        return pltpu.make_async_remote_copy(
-            src_ref=a_part.at[r, k], dst_ref=a_part.at[r, k], send_sem=xp_send.at[r, k], recv_sem=xp_recv.at[r, k],
-            device_id={"tensor": k}, device_id_type=MESH,
+    def spreads(r, count):
+        view = a_part.at[r, pl.ds(0, count)]
+        return pltpu.make_async_remote_copy(
+            src_ref=view, dst_ref=view, send_sem=xp_send.at[r], recv_sem=xp_recv.at[r],
+            device_id={"tensor": jp}, device_id_type=MESH,
         )
 
     def spread(r):
@@ -302,20 +328,18 @@
         lane = pl.ds(g * cols, cols)
         return pltpu.make_async_remote_copy(
             src_ref=a_part.at[r, to * group + g], dst_ref=a_all.at[pl.ds(2 * r, 2), z, own_rows(j), lane],
-            send_sem=xz_send.at[r, to, g], recv_sem=xz_recv.at[r, z, g], device_id={"dp": to}, device_id_type=MESH,
-        )
-
-    def lift_from(r, k, g):
-        lane = pl.ds(g * cols, cols)
-        view = a_all.at[pl.ds(2 * r, 2), k, own_rows(j), lane]
-        return pltpu.make_async_remote_copy(
-            src_ref=view, dst_ref=view, send_sem=xz_send.at[r, k, g], recv_sem=xz_recv.at[r, k, g],
-            device_id={"dp": k}, device_id_type=MESH,
+            send_sem=xz_send.at[r], recv_sem=xz_recv.at[r], device_id={"dp": to}, device_id_type=MESH,
+        )
+
+    def lifts(r):
+        view = a_part.at[r, pl.ds(0, (planes - 1) * group)]
+        return pltpu.make_async_remote_copy(
+            src_ref=view, dst_ref=view, send_sem=xz_send.at[r], recv_sem=xz_recv.at[r],
+            device_id={"dp": lax.rem(z + 1, planes)}, device_id_type=MESH,
         )
 
     def lift(r):
-        for step in range(1, members):
-            spread_from(r, lax.rem(j + step, members)).wait_recv()
+        spreads(r, members - 1).wait_recv()
         for step in range(1, planes):
             for g in range(group):
                 lift_to(r, lax.rem(z + step, planes), g).start()
@@ -323,12 +347,13 @@
             a_all[pl.ds(2 * r, 2), z, own_rows(j), pl.ds(g * cols, cols)] = a_part[r, z * group + g]
 
     def lifted(r):
-        for step in range(1, planes):
-            for g in range(group):
-                lift_from(r, lax.rem(z + step, planes), g).wait_recv()
-
-    def score(u):
-        def body(h, carry):
+        lifts(r).wait_recv()
+
+    def score(side, *which):
+        h = (z // 2 + side) % 2
+
+        def body(i, carry):
+            u = which[0] + i
             block = a_all[u, pl.ds(2 * h, 2)].reshape(2 * unit, span)
             for q in range(queries):
                 mixed = lax.dot_general(
@@ -340,7 +365,7 @@
                     )
             return carry
 
-        lax.fori_loop(0, half_planes, body, 0)
+        lax.fori_loop(0, len(which), body, 0)
 
     def loaded(*which):
         for n in which:
@@ -352,103 +377,126 @@
     og[0].relay()
     og[1].begin()
     og[0].near()
+    og[2].begin()
+    loaded(0, 4)
+    og[0].paired()
+    project_near(0)
     og[0].far()
     og[0].finish()
-    loaded(0, 4)
     project(0)
     og[1].relay()
-    og[2].begin()
+    act[0].begin()
     og[1].near()
+    og[1].paired()
+    project_near(1)
+    service(1, 0)
     og[1].far()
+    og[2].relay()
+    act[1].begin()
+    og[2].near()
     og[1].finish()
     project(1)
-    og[2].relay()
-    act[0].begin()
-    og[2].near()
-    service(1, 0)
+    service(2, 0)
+    act[0].relay()
+    act[2].begin()
+    act[0].near()
+    og[2].paired()
+    project_near(2)
     og[2].far()
     og[2].finish()
+    service(1, 1)
     project(2)
-    service(2, 0)
-    act[0].relay()
-    act[1].begin()
-    act[0].near()
-    service(1, 1)
+    service(3, 0)
+    loaded(1, 5)
+    service(2, 1)
     act[0].far()
+    act[0].paired()
     act[0].finish()
-    loaded(1, 5)
+    act[1].relay()
+    act[1].near()
     contract(0)
     spread(0)
-    act[1].relay()
-    og[3].begin()
-    service(3, 0)
-    act[1].near()
-    service(2, 1)
+    service(1, 2)
+    act[2].relay()
+    act[2].near()
+    og[3].open()
     act[1].far()
+    act[1].paired()
     act[1].finish()
     contract(1)
     spread(1)
     lift(0)
+    act[2].far()
+    act[2].paired()
+    act[2].finish()
+    contract(2)
+    spread(2)
+    og[3].extend()
     og[3].relay()
-    act[2].begin()
-    service(1, 2)
+    service(2, 2)
+    service(3, 1)
+    lift(1)
+    lift(2)
+    lifted(0)
+    acts[0].begin()
+    acts[1].begin()
     og[3].near()
-    service(3, 1)
+    og[3].paired()
+    project_near(3)
     og[3].far()
     og[3].finish()
     project(3)
-    lift(1)
-    act[2].relay()
-    lifted(0)
-    acts[0].begin()
-    act[2].near()
-    service(2, 2)
-    act[2].far()
-    act[2].finish()
-    contract(2)
-    spread(2)
     acts[0].relay()
-    acts[1].begin()
     acts[0].near()
-    acts[0].far()
-    acts[0].finish()
-    lift(2)
-    service(3, 2)
-    score(0)
-    service(1, 3)
-    acts[1].relay()
     lifted(1)
     acts[2].begin()
+    acts[1].relay()
     acts[1].near()
-    acts[1].far()
-    acts[1].finish()
-    service(2, 3)
-    score(1)
+    acts[3].begin()
+    acts[0].far()
+    acts[0].paired()
+    acts[0].finish()
+    score(0, 0)
     acts[2].relay()
-    acts[3].begin()
     acts[2].near()
-    acts[2].far()
-    acts[2].finish()
-    score(2)
-    acts[3].relay()
     lifted(2)
     acts[4].begin()
+    score(1, 0)
+    acts[1].far()
+    acts[1].paired()
+    acts[1].finish()
+    score(0, 1)
+    service(3, 2)
+    acts[3].relay()
     acts[3].near()
+    acts[5].begin()
+    service(1, 3)
+    score(1, 1)
+    acts[2].far()
+    acts[2].paired()
+    acts[2].finish()
+    score(0, 2)
+    acts[4].relay()
+    acts[4].near()
+    score(1, 2)
     acts[3].far()
+    acts[3].paired()
     acts[3].finish()
-    score(3)
-    acts[4].relay()
-    acts[5].begin()
-    acts[4].near()
-    acts[4].far()
-    acts[4].finish()
-    service(3, 3)
-    score(4)
+    score(0, 3)
+    service(2, 3)
     acts[5].relay()
     acts[5].near()
+    score(1, 3)
+    acts[4].far()
+    acts[4].paired()
+    acts[4].finish()
+    score(0, 4)
     acts[5].far()
+    acts[5].paired()
     acts[5].finish()
-    score(5)
+    score(0, 5)
+    service(3, 3)
+    score(1, 4, 5)
     per = res_ref.shape[1]
     lane_at = lax.broadcasted_iota(jnp.int32, (8, per), 1)
     for b in range(planes):
@@ -460,22 +508,22 @@
 
     def fold(to):
         return pltpu.make_async_remote_copy(
-            src_ref=tiles.at[to], dst_ref=got_z.at[z], send_sem=rz_send.at[to], recv_sem=rz_recv.at[z],
+            src_ref=tiles.at[to], dst_ref=got_z.at[z], send_sem=rz_send.at[0], recv_sem=rz_recv.at[0],
             device_id={"dp": to}, device_id_type=MESH,
         )
 
-    def fold_from(k):
-        return pltpu.make_async_remote_copy(
-            src_ref=got_z.at[k], dst_ref=got_z.at[k], send_sem=rz_send.at[k], recv_sem=rz_recv.at[k],
-            device_id={"dp": k}, device_id_type=MESH,
+    def folds():
+        view = got_z.at[pl.ds(0, planes - 1)]
+        return pltpu.make_async_remote_copy(
+            src_ref=view, dst_ref=view, send_sem=rz_send.at[0], recv_sem=rz_recv.at[0],
+            device_id={"dp": lax.rem(z + 1, planes)}, device_id_type=MESH,
         )
 
     def fold_all():
         for step in range(1, planes):
             fold(lax.rem(z + step, planes)).start()
         got_z[z] = tiles[z]
-        for step in range(1, planes):
-            fold_from(lax.rem(z + step, planes)).wait_recv()
+        folds().wait_recv()
         total = got_z[0]
         for b in range(1, planes):
             total = total + got_z[b]
@@ -483,21 +531,21 @@
 
     def share(to):
         return pltpu.make_async_remote_copy(
-            src_ref=got_p.at[j], dst_ref=got_p.at[j], send_sem=rp_send.at[to], recv_sem=rp_recv.at[j],
+            src_ref=got_p.at[j], dst_ref=got_p.at[j], send_sem=rp_send.at[0], recv_sem=rp_recv.at[0],
             device_id={"tensor": to}, device_id_type=MESH,
         )
 
-    def share_from(k):
-        return pltpu.make_async_remote_copy(
-            src_ref=got_p.at[k], dst_ref=got_p.at[k], send_sem=rp_send.at[k], recv_sem=rp_recv.at[k],
-            device_id={"tensor": k}, device_id_type=MESH,
+    def shares():
+        view = got_p.at[pl.ds(0, members - 1)]
+        return pltpu.make_async_remote_copy(
+            src_ref=view, dst_ref=view, send_sem=rp_send.at[0], recv_sem=rp_recv.at[0],
+            device_id={"tensor": jp}, device_id_type=MESH,
         )
 
     def share_all():
         for step in range(1, members):
             share(lax.rem(j + step, members)).start()
-        for step in range(1, members):
-            share_from(lax.rem(j + step, members)).wait_recv()
+        shares().wait_recv()
         total = got_p[0]
         for k in range(1, members):
             total = total + got_p[k]
@@ -507,25 +555,18 @@
         for op in og + act + acts:
             op.drain()
         for level in range(planes):
-            for n in range(len(pieces)):
-                @pl.when((z - level >= 0) & (z < planes - 1))
-                def _():
-                    up(z - level, n).wait_send()
-
-                @pl.when((z + level < planes) & (z > 0))
-                def _():
-                    down(z + level, n).wait_send()
-        for step in range(1, members):
-            to = lax.rem(j + step, members)
-            for r in range(pairs):
-                spread_to(r, to).wait_send()
-            share(to).wait_send()
-        for step in range(1, planes):
-            to = lax.rem(z + step, planes)
-            for r in range(pairs):
-                for g in range(group):
-                    lift_to(r, to, g).wait_send()
-            fold(to).wait_send()
+            @pl.when((z - level >= 0) & (z < planes - 1))
+            def _():
+                whole(z - level, up_send, up_recv).wait_send()
+
+            @pl.when((z + level < planes) & (z > 0))
+            def _():
+                whole(z + level, dn_send, dn_recv).wait_send()
+        for r in range(pairs):
+            spreads(r, members - 1).wait_send()
+            lifts(r).wait_send()
+        folds().wait_send()
+        shares().wait_send()
 
     fold_all()
     share_all()
@@ -540,6 +581,7 @@
     return (
         members == 8 and planes == 4 and rows == tokens and rows == unit * seq_count and unit == 16 * members
         and seq_count == 6 and feats % 128 == 0 and cols % 128 == 0 and span % cols == 0 and span == 2 * cols
+        and (members * width) // (6 * unit) == members // 2 * width // (6 * unit) - (-(members // 2) * width // (6 * unit))
         and width % 16 == 0 and width > 32 and query_proj.shape[0] <= 8
     )
 
@@ -584,10 +626,10 @@
             pltpu.VMEM((planes, 8, 128), f32),
             pltpu.VMEM((planes, 8, 128), f32),
             pltpu.VMEM((members, 8, 128), f32),
-            dma((6,)), dma((ops, 11)), dma((ops, 11)),
-            dma((planes, pieces)), dma((planes, pieces)), dma((planes, pieces)), dma((planes, pieces)),
-            dma((pairs, members)), dma((pairs, members)), dma((pairs, planes, group)), dma((pairs, planes, group)),
-            dma((planes,)), dma((planes,)), dma((members,)), dma((members,)),
+            dma((6,)), dma((ops,)), dma((ops, 6)),
+            dma((planes,)), dma((planes, pieces)), dma((planes,)), dma((planes, pieces)),
+            dma((pairs,)), dma((pairs,)), dma((pairs,)), dma((pairs,)),
+            dma((1,)), dma((1,)), dma((1,)), dma((1,)),
         ],
         compiler_params=pltpu.CompilerParams(
             collective_id=0, has_side_effects=True, vmem_limit_bytes=63 * 1024 * 1024

time: 155 us -> 124 us (0.80)
  Pallas kernels: 153 us -> 121 us
    pallas_call x1, Pallas kernels: 153 us -> 121 us  [local(): pl.pallas_call(kernel, out_shape=jax.ShapeDtypeStruct((8, 128), f32), in_...]
where the time goes in v2:
time: 124 us; the launch traced here: 123 us
  Pallas kernels  121 us (98%)
  other arithmetic  1.26 us (1%)
    pallas_call x1, Pallas kernels, local(): pl.pallas_call(kernel, out_shape=jax.ShapeDtypeStruct((8, 128), f32), in_...  121 us

profile of v2, /device:TPU:0, one launch (start us, length us, event | category | flops | bytes accessed | tf_op | source)
XLA Modules:
  0.0 123.3 jit_solution(10872944662647965574)
XLA Ops:
  0.7 121.4 %shard_map.82 = f32[8,128]{1,0:T(8,128)} custom-call(bf16[768,512]{1,0:T(8,128)(2,1)} %act_ref.1, bf16[688,768]{1,0:T(8,128)(2,1)} %og_ref.1, bf16[4096,512]{1,0:T(8,128)(2,1)} %in_ref.1, bf16[688,5504]{1,0:T(8,128)(2,1)} %out_ref.1, bf16[4,688,1024]{2,1,0:T(8,128)(2,1)} %query_ref.1, f32[688,1024]{1,0:T(8,128)} %eig_ref.1, s32[6]{0:T(128)} %len_ref.1, ...), custom_call_target="tpu_custom_call" | custom-call | tf_op jit(solution)/shard_map/pallas_call | solution.py:607
  122.0 1.3 %multiply_bitcast_fusion = f32[6,4]{0,1:T(4,128)} fusion(f32[8,128]{1,0:T(8,128)} %shard_map.82), kind=kLoop, calls=%fused_computation | loop fusion | flops 24 | bytes 192 | tf_op jit(solution)/shard_map/mul | solution.py:639

commit v3 on v2

--- a/solution.py
+++ b/solution.py
@@ -42,7 +42,7 @@
 def kernel(
     act_ref, og_ref, in_ref, out_ref, query_ref, eig_ref, len_ref, damp_ref, res_ref,
     og_all, act_all, in_b, out_b, scaled, eig, a_all, a_part, a_loc, a_acc, g_all, g_acc, csum, tiles, got_z, got_p,
-    load_sem, gs_send, gs_recv, up_send, up_recv, dn_send, dn_recv, xp_send, xp_recv, xz_send, xz_recv,
+    load_sem, gs_send, gs_recv, up_send, dn_send, ch_recv, xp_send, xp_recv, xz_send, xz_recv,
     rz_send, rz_recv, rp_send, rp_recv,
 ):
     bf16, f32 = jnp.bfloat16, jnp.float32
@@ -57,6 +57,7 @@
     group = span // cols
     half_planes = planes // 2
     pieces = [(0, 1), (1, 1)] + [(2 * n, 2) for n in range(1, pairs)]
+    hops = pieces[:-1] + [(units - 2, 1), (units - 1, 1)]
     jx = j + 2 - 4 * lax.rem(j // 2, 2)
     jy = j + 4 - 8 * (j // 4)
     jd = jx + 4 - 8 * (j // 4)
@@ -188,7 +189,7 @@
 
     og = [og_gather(n, *piece) for n, piece in enumerate(pieces)]
     act = [act_gather(len(og) + r, r) for r in range(pairs)]
-    acts = [acts_gather(len(og) + len(act) + u, u) for u in range(units)]
+    acts = [acts_gather(u if u < pairs else len(og) + u - pairs, u) for u in range(units)]
 
     def scale_all():
         csum[...] = jnp.zeros_like(csum)
@@ -206,7 +207,7 @@
         lax.fori_loop(0, width // step_rows, scale, 0)
 
     def chain(n, block, sends, recvs, to):
-        first, count = pieces[n]
+        first, count = hops[n]
         view = g_all.at[block, pl.ds(first, count)]
         return pltpu.make_async_remote_copy(
             src_ref=view, dst_ref=view, send_sem=sends.at[block], recv_sem=recvs.at[block, n],
@@ -220,10 +221,10 @@
         )
 
     def up(block, n):
-        return chain(n, block, up_send, up_recv, lax.rem(z + 1, planes))
+        return chain(n, block, up_send, ch_recv, lax.rem(z + 1, planes))
 
     def down(block, n):
-        return chain(n, block, dn_send, dn_recv, lax.rem(z + planes - 1, planes))
+        return chain(n, block, dn_send, ch_recv, lax.rem(z + planes - 1, planes))
 
     def service(level, n):
         @pl.when(z - level >= 0)
@@ -277,17 +278,18 @@
             )
         deepen(n, 0, k_full - k_near, (1 - upper) * k_near)
         lane = lax.broadcasted_iota(jnp.int32, (1, unit), 1)
-        for i in range(count):
-            keep = (lane < len_ref[first + i]).astype(f32)
-            g_all[z, first + i] = (g_acc[:, pl.ds(i * unit, unit)] * keep).astype(bf16)
-
-        @pl.when(z < planes - 1)
-        def _():
-            up(z, n).start()
-
-        @pl.when(z > 0)
-        def _():
-            down(z, n).start()
+        for hop in range(n, n + 1 if n < len(pieces) - 1 else len(hops)):
+            for i in range(hops[hop][0], sum(hops[hop])):
+                keep = (lane < len_ref[i]).astype(f32)
+                g_all[z, i] = (g_acc[:, pl.ds((i - first) * unit, unit)] * keep).astype(bf16)
+
+            @pl.when(z < planes - 1)
+            def _():
+                up(z, hop).start()
+
+            @pl.when(z > 0)
+            def _():
+                down(z, hop).start()
 
     def contract(r):
         at = pl.ds(2 * unit * r, 2 * unit)
@@ -438,7 +440,9 @@
     lift(1)
     lift(2)
     lifted(0)
+    og[0].drain()
     acts[0].begin()
+    og[1].drain()
     acts[1].begin()
     og[3].near()
     og[3].paired()
@@ -449,10 +453,12 @@
     acts[0].relay()
     acts[0].near()
     lifted(1)
+    og[2].drain()
     acts[2].begin()
     acts[1].relay()
+    act[0].drain()
+    acts[3].begin()
     acts[1].near()
-    acts[3].begin()
     acts[0].far()
     acts[0].paired()
     acts[0].finish()
@@ -460,43 +466,49 @@
     acts[2].relay()
     acts[2].near()
     lifted(2)
+    act[1].drain()
     acts[4].begin()
+    acts[1].far()
     score(1, 0)
-    acts[1].far()
+    service(1, 3)
     acts[1].paired()
     acts[1].finish()
     score(0, 1)
-    service(3, 2)
     acts[3].relay()
     acts[3].near()
+    act[2].drain()
     acts[5].begin()
-    service(1, 3)
+    acts[2].far()
+    service(1, 4)
     score(1, 1)
-    acts[2].far()
     acts[2].paired()
     acts[2].finish()
     score(0, 2)
     acts[4].relay()
     acts[4].near()
+    acts[3].far()
+    service(3, 2)
     score(1, 2)
-    acts[3].far()
+    service(2, 3)
     acts[3].paired()
     acts[3].finish()
     score(0, 3)
-    service(2, 3)
     acts[5].relay()
     acts[5].near()
+    acts[4].far()
+    service(2, 4)
     score(1, 3)
-    acts[4].far()
     acts[4].paired()
     acts[4].finish()
     score(0, 4)
     acts[5].far()
+    service(3, 3)
+    score(1, 4)
     acts[5].paired()
     acts[5].finish()
     score(0, 5)
-    service(3, 3)
-    score(1, 4, 5)
+    service(3, 4)
+    score(1, 5)
     per = res_ref.shape[1]
     lane_at = lax.broadcasted_iota(jnp.int32, (8, per), 1)
     for b in range(planes):
@@ -552,16 +564,16 @@
         res_ref[...] = total
 
     def drain_all():
-        for op in og + act + acts:
+        for op in og[pairs:] + acts:
             op.drain()
         for level in range(planes):
             @pl.when((z - level >= 0) & (z < planes - 1))
             def _():
-                whole(z - level, up_send, up_recv).wait_send()
+                whole(z - level, up_send, ch_recv).wait_send()
 
             @pl.when((z + level < planes) & (z > 0))
             def _():
-                whole(z + level, dn_send, dn_recv).wait_send()
+                whole(z + level, dn_send, ch_recv).wait_send()
         for r in range(pairs):
             spreads(r, members - 1).wait_send()
             lifts(r).wait_send()
@@ -599,7 +611,7 @@
     unit = rows // seq_count
     part, pairs, group = unit // members, seq_count // 2, span // cols
     pieces = pairs + 1
-    ops = pieces + pairs + seq_count
+    ops = pieces + pairs
     any_space = pl.BlockSpec(memory_space=pl.ANY)
     vmem = pl.BlockSpec(memory_space=pltpu.VMEM)
     smem = pl.BlockSpec(memory_space=pltpu.SMEM)
@@ -627,7 +639,7 @@
             pltpu.VMEM((planes, 8, 128), f32),
             pltpu.VMEM((members, 8, 128), f32),
             dma((6,)), dma((ops,)), dma((ops, 6)),
-            dma((planes,)), dma((planes, pieces)), dma((planes,)), dma((planes, pieces)),
+            dma((planes,)), dma((planes,)), dma((planes, pieces + 1)),
             dma((pairs,)), dma((pairs,)), dma((pairs,)), dma((pairs,)),
             dma((1,)), dma((1,)), dma((1,)), dma((1,)),
         ],

time: 124 us -> 119 us (0.960)
  Pallas kernels: 121 us -> 117 us
    pallas_call x1, Pallas kernels: 121 us -> 117 us  [local(): pl.pallas_call(kernel, out_shape=jax.ShapeDtypeStruct((8, 128), f32), in_...]
where the time goes in v3:
time: 119 us
  Pallas kernels  117 us (98%)
  other arithmetic  1.26 us (1%)
    pallas_call x1, Pallas kernels, local(): pl.pallas_call(kernel, out_shape=jax.ShapeDtypeStruct((8, 128), f32), in_...  117 us

profile of v3, /device:TPU:0, one launch (start us, length us, event | category | flops | bytes accessed | tf_op | source)
XLA Modules:
  0.0 119.1 jit_solution(10045256480416813028)
XLA Ops:
  0.7 117.2 %shard_map.82 = f32[8,128]{1,0:T(8,128)} custom-call(bf16[768,512]{1,0:T(8,128)(2,1)} %act_ref.1, bf16[688,768]{1,0:T(8,128)(2,1)} %og_ref.1, bf16[4096,512]{1,0:T(8,128)(2,1)} %in_ref.1, bf16[688,5504]{1,0:T(8,128)(2,1)} %out_ref.1, bf16[4,688,1024]{2,1,0:T(8,128)(2,1)} %query_ref.1, f32[688,1024]{1,0:T(8,128)} %eig_ref.1, s32[6]{0:T(128)} %len_ref.1, ...), custom_call_target="tpu_custom_call" | custom-call | tf_op jit(solution)/shard_map/pallas_call | solution.py:619
  117.9 1.3 %multiply_bitcast_fusion = f32[6,4]{0,1:T(4,128)} fusion(f32[8,128]{1,0:T(8,128)} %shard_map.82), kind=kLoop, calls=%fused_computation | loop fusion | flops 24 | bytes 192 | tf_op jit(solution)/shard_map/mul | solution.py:651

commit v4 on v3

--- a/solution.py
+++ b/solution.py
@@ -434,42 +434,42 @@
     contract(2)
     spread(2)
     og[3].extend()
-    og[3].relay()
     service(2, 2)
     service(3, 1)
     lift(1)
-    lift(2)
     lifted(0)
     og[0].drain()
     acts[0].begin()
-    og[1].drain()
-    acts[1].begin()
+    og[3].relay()
+    lift(2)
     og[3].near()
     og[3].paired()
     project_near(3)
+    acts[0].relay()
+    og[1].drain()
+    acts[1].begin()
+    acts[0].near()
     og[3].far()
-    og[3].finish()
-    project(3)
-    acts[0].relay()
-    acts[0].near()
     lifted(1)
     og[2].drain()
     acts[2].begin()
+    og[3].finish()
+    acts[0].far()
+    project(3)
+    acts[0].paired()
+    acts[0].finish()
     acts[1].relay()
+    score(0, 0)
     act[0].drain()
     acts[3].begin()
     acts[1].near()
-    acts[0].far()
-    acts[0].paired()
-    acts[0].finish()
-    score(0, 0)
+    score(1, 0)
     acts[2].relay()
     acts[2].near()
     lifted(2)
     act[1].drain()
     acts[4].begin()
     acts[1].far()
-    score(1, 0)
     service(1, 3)
     acts[1].paired()
     acts[1].finish()

time: 119 us -> 119 us (level)
  no operation moved by 1% of the time
where the time goes in v4:
time: 119 us
  Pallas kernels  117 us (98%)
  other arithmetic  1.26 us (1%)
    pallas_call x1, Pallas kernels, local(): pl.pallas_call(kernel, out_shape=jax.ShapeDtypeStruct((8, 128), f32), in_...  117 us

profile of v4, /device:TPU:0, one launch (start us, length us, event | category | flops | bytes accessed | tf_op | source)
XLA Modules:
  0.0 119.1 jit_solution(16913343500288577701)
XLA Ops:
  0.7 117.1 %shard_map.82 = f32[8,128]{1,0:T(8,128)} custom-call(bf16[768,512]{1,0:T(8,128)(2,1)} %act_ref.1, bf16[688,768]{1,0:T(8,128)(2,1)} %og_ref.1, bf16[4096,512]{1,0:T(8,128)(2,1)} %in_ref.1, bf16[688,5504]{1,0:T(8,128)(2,1)} %out_ref.1, bf16[4,688,1024]{2,1,0:T(8,128)(2,1)} %query_ref.1, f32[688,1024]{1,0:T(8,128)} %eig_ref.1, s32[6]{0:T(128)} %len_ref.1, ...), custom_call_target="tpu_custom_call" | custom-call | tf_op jit(solution)/shard_map/pallas_call | solution.py:619
  117.8 1.3 %multiply_bitcast_fusion = f32[6,4]{0,1:T(4,128)} fusion(f32[8,128]{1,0:T(8,128)} %shard_map.82), kind=kLoop, calls=%fused_computation | loop fusion | flops 24 | bytes 192 | tf_op jit(solution)/shard_map/mul | solution.py:651
